TPU v7x, 512 devices: a whole 4x4x16 slice. The times are simulated.
512 devices in a mesh: ctx: 64 (over z, y), dp: 8 (over x, core).
Axes of the slice: x: 4, y: 4, z: 16, core: 2. Of those that a mesh axis runs over, the one named last changes fastest.
Arguments:
- q_in: bfloat16 [8, 8192, 2048], P('dp', 'ctx'), may hold values from -6 to 6
- k_in: bfloat16 [8, 8192, 2048], P('dp', 'ctx'), may hold values from -6 to 6
- v_in: bfloat16 [8, 8192, 2048], P('dp', 'ctx'), may hold values from -6 to 6
- grad_out: bfloat16 [8, 8192, 2048], P('dp', 'ctx'), may hold values from -6 to 6
- short_filter: float32 [3, 3, 2048], replicated, may hold values from -3.5 to 3.5
- residue: float32 [2048, 8], replicated, may hold values from -2 to 2
- rate: float32 [8], replicated, may hold values from 0.00012207031 to 0.1
Outputs:
- mixed: bfloat16 [8, 8192, 2048], P('dp', 'ctx')
- grad_q: bfloat16 [8, 8192, 2048], P('dp', 'ctx')
- grad_k: bfloat16 [8, 8192, 2048], P('dp', 'ctx')
- grad_v: bfloat16 [8, 8192, 2048], P('dp', 'ctx')
- grad_residue: float32 [2048, 8], P('ctx')
- grad_short: float32 [3, 3, 2048], replicated
All inputs are finite; a program needn't handle non-finite values.
Results may differ from a plain program's by a relative error of at most 0.024.
Values may be sent and summed in bfloat16 or wider, within the bound.
A program may use at most 64 MiB of HBM per device.

v0:
```python
import jax
import jax.numpy as jnp
from jax import lax
from jax.sharding import PartitionSpec as P

BLOCK = 128
PRECISE = lax.Precision.HIGHEST


def passed_along(block, axis, distance):
    devices = range(lax.axis_size(axis))
    route = [(i - distance, i) for i in devices if i - distance in devices]
    return lax.ppermute(block, axis, route)


def mode_sweeps(source, cotangent, rates, columns, gains, front, behind):
    block_len = BLOCK
    block_count = source.shape[1]
    places = jnp.arange(block_len, dtype=jnp.float32)
    offset = places[:, None] - places[None, :]
    blocks = jnp.arange(block_count, dtype=jnp.float32)
    spacing = blocks[:, None] - blocks[None, :] - 1.0
    cot_f = cotangent.astype(jnp.float32)

    def one_mode(carry, item):
        conv_acc, back_acc = carry
        speed, column, start_fwd, start_back = item
        kernel = jnp.where(offset >= 0, jnp.exp(-speed * jnp.maximum(offset, 0.0)), 0.0).astype(
            jnp.bfloat16
        )
        passing = jnp.where(
            spacing >= 0, jnp.exp(-speed * block_len * jnp.maximum(spacing, 0.0)), 0.0
        )
        lead = jnp.exp(-speed * block_len * blocks)
        trail = jnp.exp(-speed * block_len * (block_count - 1.0 - blocks))
        scale_fwd = jnp.exp(-speed * (places + 1.0))
        scale_back = jnp.exp(-speed * (block_len - places))
        inside = jnp.einsum("ts,cns->cnt", kernel, source, preferred_element_type=jnp.float32)
        entering = (
            jnp.einsum("nk,ck->cn", passing, inside[..., block_len - 1], precision=PRECISE)
            + lead[None, :] * start_fwd[:, None]
        )
        forward = inside + scale_fwd[None, None, :] * entering[..., None]
        conv_acc = conv_acc + column[:, None, None] * forward
        grad_row = jnp.sum(forward * cot_f, axis=(1, 2))
        inside_back = jnp.einsum(
            "ts,cnt->cns", kernel, cotangent, preferred_element_type=jnp.float32
        )
        entering_back = (
            jnp.einsum("kn,ck->cn", passing, inside_back[..., 0], precision=PRECISE)
            + trail[None, :] * start_back[:, None]
        )
        backward = inside_back + scale_back[None, None, :] * entering_back[..., None]
        back_acc = back_acc + column[:, None, None] * backward
        return ((conv_acc, back_acc), grad_row)

    zeros_acc = jnp.zeros(source.shape, jnp.float32)
    (conv_sum, back_sum), grads = lax.scan(
        one_mode, (zeros_acc, zeros_acc), (rates, columns, front, behind)
    )
    grads = gains[:, None] * grads
    return (conv_sum, back_sum, grads.T)


def shards(q_in, k_in, v_in, grad_out, short_filter, residue, rate):
    row_count = q_in.shape[1]
    width = q_in.shape[2]
    inputs = (q_in[0], k_in[0], v_in[0])
    tails = jnp.stack([item[row_count - 2 :] for item in inputs])
    before = passed_along(tails, "ctx", 1)
    extended = [
        jnp.concatenate([before[branch], inputs[branch]], axis=0).astype(jnp.float32)
        for branch in range(3)
    ]
    shorts = []
    for branch in range(3):
        total = short_filter[branch, 0][None, :] * extended[branch][2 : 2 + row_count]
        for tap_at in range(1, 3):
            total = (
                total
                + short_filter[branch, tap_at][None, :]
                * extended[branch][2 - tap_at : 2 - tap_at + row_count]
            )
        shorts.append(total)
    query, keyed, valued = shorts
    gated = (keyed * valued).astype(jnp.bfloat16)
    cot_out = grad_out[0].astype(jnp.float32)
    d_conv = (cot_out * query).astype(jnp.bfloat16)
    gains = jnp.sqrt(1.0 - jnp.exp(-2.0 * rate))
    weights = residue * gains[None, :]
    modes = rate.shape[0]
    ctx_count = lax.axis_size("ctx")
    channel_share = width // ctx_count
    owned, incoming = (
        lax.all_to_all(gated, "ctx", split_axis=1, concat_axis=0, tiled=True),
        lax.all_to_all(d_conv, "ctx", split_axis=1, concat_axis=0, tiled=True),
    )
    total_rows = owned.shape[0]
    block_count = total_rows // BLOCK
    owned_lanes = owned.T.reshape(channel_share, block_count, BLOCK)
    incoming_lanes = incoming.T.reshape(channel_share, block_count, BLOCK)
    columns = lax.dynamic_slice_in_dim(
        weights, lax.axis_index("ctx") * channel_share, channel_share, 0
    ).T
    zero_start = jnp.zeros((modes, channel_share), jnp.float32)
    conv_sum, back_sum, partial_value = mode_sweeps(
        owned_lanes, incoming_lanes, rate, columns, gains, zero_start, zero_start
    )
    conv_rows = conv_sum.reshape(channel_share, total_rows).T.astype(jnp.bfloat16)
    back_rows = back_sum.reshape(channel_share, total_rows).T.astype(jnp.bfloat16)
    conv, d_gated = (
        lax.all_to_all(conv_rows, "ctx", split_axis=0, concat_axis=1, tiled=True),
        lax.all_to_all(back_rows, "ctx", split_axis=0, concat_axis=1, tiled=True),
    )
    grad_residue = lax.psum(partial_value, "dp")
    conv_f = conv.astype(jnp.float32)
    mixed = (query * conv_f).astype(jnp.bfloat16)
    gated_back = d_gated.astype(jnp.float32)
    d_shorts = (cot_out * conv_f, gated_back * valued, gated_back * keyed)
    heads = jnp.stack([item[:2] for item in d_shorts])
    after = passed_along(heads.astype(jnp.bfloat16), "ctx", -1).astype(heads.dtype)
    grads = []
    partial_short = []
    for branch in range(3):
        ahead_rows = jnp.concatenate([d_shorts[branch], after[branch]], axis=0)
        total = short_filter[branch, 0][None, :] * ahead_rows[0:row_count]
        for tap_at in range(1, 3):
            total = (
                total
                + short_filter[branch, tap_at][None, :] * ahead_rows[tap_at : tap_at + row_count]
            )
        grads.append(total.astype(jnp.bfloat16)[None])
        partial_short.append(
            jnp.stack(
                [
                    jnp.sum(
                        d_shorts[branch] * extended[branch][2 - tap_at : 2 - tap_at + row_count],
                        axis=0,
                    )
                    for tap_at in range(3)
                ]
            )
        )
    grad_short = lax.psum(jnp.stack(partial_short), ("ctx", "dp"))
    return (mixed[None], grads[0], grads[1], grads[2], grad_residue, grad_short)


def solution(mesh):
    placed = (
        P("dp", "ctx", None),
        P("dp", "ctx", None),
        P("dp", "ctx", None),
        P("dp", "ctx", None),
        P(),
        P(),
        P(),
    )
    return jax.shard_map(
        shards,
        mesh=mesh,
        in_specs=placed,
        out_specs=(
            P("dp", "ctx", None),
            P("dp", "ctx", None),
            P("dp", "ctx", None),
            P("dp", "ctx", None),
            P("ctx", None),
            P(),
        ),
        check_vma=False,
    )
```

profile of v0, /device:TPU:1, one launch (start us, length us, event | category | flops | bytes accessed | tf_op | source)
XLA Modules:
  0.0 703.1 jit_solution(16576350189797462453)
XLA Ops:
  9.5 4.0 collective-permute-start
  18.7 4.5 multiply_convert_fusion
  23.2 18.3 %all-to-all-start = ((bf16[128,64,32]{0,2,1:T(8,128)(2,1)}), bf16[128,64,32]{0,2,1:T(8,128)(2,1)S(1)}, u32[]{:S(2)}, u32[]{:S(2)}) async-start(bf16[128,64,32]{0,2,1:T(8,128)(2,1)} %bitcast.16), calls=%async_computation | async-start | bytes 1048576 | tf_op jit(solution)/shard_map/all_to_all | solution.py:95
  44.2 2.4 fusion.51
  46.6 24.2 %all-to-all-done = bf16[128,64,32]{0,2,1:T(8,128)(2,1)S(1)} async-done(((bf16[128,64,32]{0,2,1:T(8,128)(2,1)}), bf16[128,64,32]{0,2,1:T(8,128)(2,1)S(1)}, u32[]{:S(2)}, u32[]{:S(2)}) %all-to-all-start) | async-done | bytes 524320 | tf_op jit(solution)/shard_map/all_to_all | solution.py:95
  70.7 8.6 %all-to-all-start.1 = ((bf16[128,64,32]{0,2,1:T(8,128)(2,1)}), bf16[128,64,32]{0,2,1:T(8,128)(2,1)S(1)}, u32[]{:S(2)}, u32[]{:S(2)}) async-start(bf16[128,64,32]{0,2,1:T(8,128)(2,1)} %bitcast.20), calls=%async_computation.1 | async-start | bytes 1048576 | tf_op jit(solution)/shard_map/all_to_all | solution.py:96
  81.2 27.1 %all-to-all-done.1 = bf16[128,64,32]{0,2,1:T(8,128)(2,1)S(1)} async-done(((bf16[128,64,32]{0,2,1:T(8,128)(2,1)}), bf16[128,64,32]{0,2,1:T(8,128)(2,1)S(1)}, u32[]{:S(2)}, u32[]{:S(2)}) %all-to-all-start.1) | async-done | bytes 524320 | tf_op jit(solution)/shard_map/all_to_all | solution.py:96
  110.5 60.8 %while.16 = (s32[]{:T(128)}, f32[32,64,128]{2,1,0:T(8,128)}, f32[32,64,128]{2,1,0:T(8,128)}, f32[8,32]{1,0:T(8,128)S(1)}, f32[8,32]{1,0:T(8,128)S(1)}, /*index=5...) while((s32[]{:T(128)}, f32[32,64,128]{2,1,0:T(8,128)}, ...), condition=%wide.region_2.3_spmd.clone.clone, body=%wide.region_0.2_spmd.clone.clone.sunk | while | flops 140759840 | bytes 12668891 | solution.py:58
  121.5 3.3 multiply_reduce_fusion.11
  129.2 3.3 multiply_reduce_fusion.11
  137.0 3.3 multiply_reduce_fusion.11
  144.7 3.3 multiply_reduce_fusion.11
  152.5 3.3 multiply_reduce_fusion.11
  160.2 3.3 multiply_reduce_fusion.11
  167.9 3.3 multiply_reduce_fusion.11
  173.8 9.2 %all-to-all-start.3 = ((bf16[64,128,32]{1,2,0:T(8,128)(2,1)}), bf16[64,128,32]{1,2,0:T(8,128)(2,1)}, u32[]{:S(2)}, u32[]{:S(2)}) async-start(bf16[64,128,32]{1,2,0:T(8,128)(2,1)} %copy_bitcast_fusion), calls=%async_computation.3 | async-start | bytes 1048576 | tf_op jit(solution)/shard_map/all_to_all | solution.py:113
  184.3 27.9 %all-to-all-done.3 = bf16[64,128,32]{1,2,0:T(8,128)(2,1)} async-done(((bf16[64,128,32]{1,2,0:T(8,128)(2,1)}), bf16[64,128,32]{1,2,0:T(8,128)(2,1)}, u32[]{:S(2)}, u32[]{:S(2)}) %all-to-all-start.3) | async-done | bytes 524320 | tf_op jit(solution)/shard_map/all_to_all | solution.py:113
  212.1 8.9 %all-to-all-start.2 = ((bf16[64,128,32]{1,2,0:T(8,128)(2,1)}), bf16[64,128,32]{1,2,0:T(8,128)(2,1)}, u32[]{:S(2)}, u32[]{:S(2)}) async-start(bf16[64,128,32]{1,2,0:T(8,128)(2,1)} %copy_bitcast_fusion.1), calls=%async_computation.2 | async-start | bytes 1048576 | tf_op jit(solution)/shard_map/all_to_all | solution.py:112
  221.2 14.6 %psum.14 = f32[32,8]{0,1:T(8,128)} all-reduce(f32[32,8]{0,1:T(8,128)S(1)} %multiply_bitcast_fusion), channel_id=1, replica_groups=mesh['ctx'=64,'dp'=8] {'dp'}, use_global_device_ids=true, to_apply=%region_3.4 | all-reduce | flops 256 | bytes 2048 | tf_op jit(solution)/shard_map/psum | solution.py:115
  235.8 6.3 multiply_reduce_fusion.6
  247.3 2.9 all-to-all-done.2
  250.2 3.0 multiply_reduce_fusion.9
  262.6 2.2 fusion.75
  270.0 424.7 %all-reduce.2.cloned.1.call-done = f32[3,3,2048]{2,1,0:T(4,128)} async-done(((f32[3,3,2048]{2,1,0:T(4,128)}), f32[3,3,2048]{2,1,0:T(4,128)}) %all-reduce.2.cloned.1.call-update) | async-done | bytes 73744 | tf_op jit(solution)/shard_map/psum | solution.py:144
  (191 shorter events, 70.8 us)
Async XLA Ops:
  9.5 7.7 %collective-permute-start = (bf16[3,2,2048]{2,1,0:T(2,128)(2,1)S(1)}, bf16[3,2,2048]{2,1,0:T(2,128)(2,1)S(1)}, u32[]{:S(2)}, u32[]{:S(2)}) collective-permute-start(bf16[3,2,2048]{2,1,0:T(2,128)(2,1)S(1)} %pad_maximum_fusion.4), channel_id=1, source_target_pairs={{0,8},{8,16},{16,24},{24,32},{32,40},{40,48},{48,56},{56,64},{64,7... | collective-permute-start | bytes 73736 | tf_op jit(solution)/shard_map/ppermute | solution.py:13
  18.7 4.5 copy-start.1
  18.7 4.5 copy-start.3
  18.7 22.8 %copy-start.13 = (bf16[1,128,2048]{2,1,0:T(8,128)(2,1)S(1)}, bf16[1,128,2048]{2,1,0:T(8,128)(2,1)}, u32[]{:S(2)}) copy-start(bf16[1,128,2048]{2,1,0:T(8,128)(2,1)} %param.9) | copy-start | bytes 1572868
  23.2 18.6 %copy-start.14 = (bf16[1,128,2048]{2,1,0:T(8,128)(2,1)S(1)}, bf16[1,128,2048]{2,1,0:T(8,128)(2,1)}, u32[]{:S(2)}) copy-start(bf16[1,128,2048]{2,1,0:T(8,128)(2,1)} %param.12) | copy-start | bytes 1572868
  23.2 47.5 %all-to-all-start = ((bf16[128,64,32]{0,2,1:T(8,128)(2,1)}), bf16[128,64,32]{0,2,1:T(8,128)(2,1)S(1)}, u32[]{:S(2)}, u32[]{:S(2)}) async-start(bf16[128,64,32]{0,2,1:T(8,128)(2,1)} %bitcast.16), calls=%async_computation | async-start | bytes 1048576 | tf_op jit(solution)/shard_map/all_to_all | solution.py:95
  42.1 4.5 copy-start.11
  44.2 35.2 %copy-start.15 = (f32[8]{0:T(128)S(1)}, f32[8]{0:T(128)}, u32[]{:S(2)}) copy-start(f32[8]{0:T(128)} %param.15) | copy-start | bytes 100
  70.7 37.6 %all-to-all-start.1 = ((bf16[128,64,32]{0,2,1:T(8,128)(2,1)}), bf16[128,64,32]{0,2,1:T(8,128)(2,1)S(1)}, u32[]{:S(2)}, u32[]{:S(2)}) async-start(bf16[128,64,32]{0,2,1:T(8,128)(2,1)} %bitcast.20), calls=%async_computation.1 | async-start | bytes 1048576 | tf_op jit(solution)/shard_map/all_to_all | solution.py:96
  111.7 2.0 copy-start.6
  118.3 2.0 copy-start.6
  133.8 2.0 copy-start.6
  157.0 2.0 copy-start.6
  164.8 2.0 copy-start.6
  171.3 11.8 %copy-start = (f32[32,64,128]{2,1,0:T(8,128)S(1)}, f32[32,64,128]{2,1,0:T(8,128)}, u32[]{:S(2)}) copy-start(f32[32,64,128]{2,1,0:T(8,128)} %get-tuple-element.87) | copy-start | bytes 3145732
  173.8 38.3 %all-to-all-start.3 = ((bf16[64,128,32]{1,2,0:T(8,128)(2,1)}), bf16[64,128,32]{1,2,0:T(8,128)(2,1)}, u32[]{:S(2)}, u32[]{:S(2)}) async-start(bf16[64,128,32]{1,2,0:T(8,128)(2,1)} %copy_bitcast_fusion), calls=%async_computation.3 | async-start | bytes 1048576 | tf_op jit(solution)/shard_map/all_to_all | solution.py:113
  183.0 52.7 %copy-start.2 = (f32[130,2048]{0,1:T(8,128)S(1)}, f32[130,2048]{0,1:T(8,128)}, u32[]{:S(2)}) copy-start(f32[130,2048]{0,1:T(8,128)} %copy-done.1) | copy-start | bytes 3194884
  212.1 38.0 %all-to-all-start.2 = ((bf16[64,128,32]{1,2,0:T(8,128)(2,1)}), bf16[64,128,32]{1,2,0:T(8,128)(2,1)}, u32[]{:S(2)}, u32[]{:S(2)}) async-start(bf16[64,128,32]{1,2,0:T(8,128)(2,1)} %copy_bitcast_fusion.1), calls=%async_computation.2 | async-start | bytes 1048576 | tf_op jit(solution)/shard_map/all_to_all | solution.py:112
  221.0 473.7 %all-reduce.2.cloned.1.call-start = ((), (), s32[]{:S(2)}) async-start(), calls=%async_computation.4 | async-start | bytes 196608 | tf_op jit(solution)/shard_map/psum | solution.py:144
  242.1 8.1 %copy-start.9 = (f32[128,2048]{0,1:T(8,128)}, f32[128,2048]{0,1:T(8,128)S(1)}, u32[]{:S(2)}) copy-start(f32[128,2048]{0,1:T(8,128)S(1)} %get-tuple-element.228) | copy-start | bytes 3145732
  242.1 8.0 %copy-start.5 = (f32[130,2048]{0,1:T(8,128)S(1)}, f32[130,2048]{0,1:T(8,128)}, u32[]{:S(2)}) copy-start(f32[130,2048]{0,1:T(8,128)} %copy-done.4) | copy-start | bytes 3194884
  253.2 2.4 copy-start.12
  253.5 4.6 collective-permute-start.1
  259.4 3.2 copy-start.8
  (6 other events, 9.4 us)
Sparse Core Ops, SparseCore 0:
  255.7 438.9 all-reduce.1
where the time goes:
time: 705 us; the launch traced here: 703 us
  waiting for transfers between devices  508 us (72%)
  other arithmetic  54 us (8%)
  starting transfers between devices  50.4 us (7%)
  local copies, waits for them, and re-layouts  39.1 us (6%)
  matrix products  16.5 us (2%)
  blocking collectives  14.6 us (2%)
  between operations  14.5 us (2%)
    psum x1, waiting for transfers between devices, shards(): grad_short = lax.psum(jnp.stack(partial_short), ('ctx', 'dp'))  425 us
    all_to_all x1, waiting for transfers between devices, shards(): lax.all_to_all(back_rows, 'ctx', split_axis=0, concat_axis=1, tiled=True)  27.9 us
    all_to_all x1, waiting for transfers between devices, shards(): lax.all_to_all(d_conv, 'ctx', split_axis=1, concat_axis=0, tiled=True)  27.1 us
    reduce_sum x8, other arithmetic, one_mode(): grad_row = jnp.sum(forward * cot_f, axis=(1, 2))  25.3 us
    all_to_all x1, waiting for transfers between devices, shards(): lax.all_to_all(gated, 'ctx', split_axis=1, concat_axis=0, tiled=True)  24.2 us
    all_to_all x1, starting transfers between devices, shards(): lax.all_to_all(gated, 'ctx', split_axis=1, concat_axis=0, tiled=True)  18.3 us
    unnamed x46, local copies, waits for them, and re-layouts  15 us
    psum x1, blocking collectives, shards(): grad_residue = lax.psum(partial_value, 'dp')  14.6 us
  transfers between devices with their start and end apart: 7, of which 6 were waited for; matrix products, arithmetic and copies ran while one was open for 5% of the time, Pallas kernels for 0%

commit v1 on v0

--- a/solution.py
+++ b/solution.py
@@ -141,7 +141,7 @@
                 ]
             )
         )
-    grad_short = lax.psum(jnp.stack(partial_short), ("ctx", "dp"))
+    grad_short = jnp.sum(lax.all_gather(jnp.stack(partial_short), ("ctx", "dp")), axis=0)
     return (mixed[None], grads[0], grads[1], grads[2], grad_residue, grad_short)
 
 

time: 705 us -> 547 us (0.78)
  waiting for transfers between devices: 508 us -> 321 us
  local copies, waits for them, and re-layouts: 39.1 us -> 51 us
  matrix products: 16.5 us -> 25.1 us
  other arithmetic: 54 us -> 61.1 us
    psum x1 -> x0, waiting for transfers between devices: 425 us -> none  [shards(): grad_short = lax.psum(jnp.stack(partial_short), ('ctx', 'dp'))]
    all_gather x0 -> x1, waiting for transfers between devices: none -> 219 us  [shards(): lax.all_gather(jnp.stack(partial_short), ('ctx', 'dp'))]
    all_to_all x1, waiting for transfers between devices: 2.88 us -> 22.9 us  [shards(): lax.all_to_all(conv_rows, 'ctx', split_axis=0, concat_axis=1, tiled=True)]
    reduce_sum x0 -> x1, other arithmetic: none -> 17.2 us  [shards(): jnp.sum(lax.all_gather(jnp.stack(partial_short), ('ctx', 'dp')), axis=0)]
    reduce_sum x8, other arithmetic: 25.3 us -> 10.9 us  [one_mode(): grad_row = jnp.sum(forward * cot_f, axis=(1, 2))]
    dot_general x8, matrix products: 2.49 us -> 10.9 us  [one_mode(): jnp.einsum('ts,cns->cnt', kernel, source, preferred_element_type=jnp.floa...]
    while x16 -> x32, local copies, waits for them, and re-layouts: 0.05 us -> 7.78 us
    unnamed x46 -> x41, local copies, waits for them, and re-layouts: 15 us -> 15.3 us
  transfers between devices with their start and end apart: 7 -> 7, of which waited for: 6 -> 5; matrix products, arithmetic and copies ran while one was open for 5% -> 8% of each run, Pallas kernels for 0% -> 0%
where the time goes in v1:
time: 547 us; the launch traced here: 545 us
  waiting for transfers between devices  321 us (59%)
  other arithmetic  61.1 us (11%)
  local copies, waits for them, and re-layouts  51 us (9%)
  starting transfers between devices  50.1 us (9%)
  matrix products  25.1 us (5%)
  blocking collectives  16.8 us (3%)
  between operations  14.4 us (3%)
  loops' own time  5.95 us (1%)
    all_gather x1, waiting for transfers between devices, shards(): lax.all_gather(jnp.stack(partial_short), ('ctx', 'dp'))  219 us
    all_to_all x1, waiting for transfers between devices, shards(): lax.all_to_all(back_rows, 'ctx', split_axis=0, concat_axis=1, tiled=True)  27.9 us
    all_to_all x1, waiting for transfers between devices, shards(): lax.all_to_all(d_conv, 'ctx', split_axis=1, concat_axis=0, tiled=True)  27.1 us
    all_to_all x1, waiting for transfers between devices, shards(): lax.all_to_all(gated, 'ctx', split_axis=1, concat_axis=0, tiled=True)  24.2 us
    all_to_all x1, waiting for transfers between devices, shards(): lax.all_to_all(conv_rows, 'ctx', split_axis=0, concat_axis=1, tiled=True)  22.9 us
    all_to_all x1, starting transfers between devices, shards(): lax.all_to_all(gated, 'ctx', split_axis=1, concat_axis=0, tiled=True)  18.3 us
    reduce_sum x1, other arithmetic, shards(): jnp.sum(lax.all_gather(jnp.stack(partial_short), ('ctx', 'dp')), axis=0)  17.2 us
    psum x1, blocking collectives, shards(): grad_residue = lax.psum(partial_value, 'dp')  16.8 us
  transfers between devices with their start and end apart: 7, of which 5 were waited for; matrix products, arithmetic and copies ran while one was open for 8% of the time, Pallas kernels for 0%

profile of v1, /device:TPU:1, one launch (start us, length us, event | category | flops | bytes accessed | tf_op | source)
XLA Modules:
  0.0 545.3 jit_solution(146845162191042597)
XLA Ops:
  9.5 4.0 collective-permute-start
  18.7 4.5 multiply_convert_fusion
  23.2 18.3 %all-to-all-start = ((bf16[128,64,32]{0,2,1:T(8,128)(2,1)}), bf16[128,64,32]{0,2,1:T(8,128)(2,1)S(1)}, u32[]{:S(2)}, u32[]{:S(2)}) async-start(bf16[128,64,32]{0,2,1:T(8,128)(2,1)} %bitcast.16), calls=%async_computation | async-start | bytes 1048576 | tf_op jit(solution)/shard_map/all_to_all | solution.py:95
  44.2 2.4 fusion.51
  46.6 24.2 %all-to-all-done = bf16[128,64,32]{0,2,1:T(8,128)(2,1)S(1)} async-done(((bf16[128,64,32]{0,2,1:T(8,128)(2,1)}), bf16[128,64,32]{0,2,1:T(8,128)(2,1)S(1)}, u32[]{:S(2)}, u32[]{:S(2)}) %all-to-all-start) | async-done | bytes 524320 | tf_op jit(solution)/shard_map/all_to_all | solution.py:95
  70.8 8.6 %all-to-all-start.1 = ((bf16[128,64,32]{0,2,1:T(8,128)(2,1)}), bf16[128,64,32]{0,2,1:T(8,128)(2,1)S(1)}, u32[]{:S(2)}, u32[]{:S(2)}) async-start(bf16[128,64,32]{0,2,1:T(8,128)(2,1)} %bitcast.20), calls=%async_computation.1 | async-start | bytes 1048576 | tf_op jit(solution)/shard_map/all_to_all | solution.py:96
  81.2 27.1 %all-to-all-done.1 = bf16[128,64,32]{0,2,1:T(8,128)(2,1)S(1)} async-done(((bf16[128,64,32]{0,2,1:T(8,128)(2,1)}), bf16[128,64,32]{0,2,1:T(8,128)(2,1)S(1)}, u32[]{:S(2)}, u32[]{:S(2)}) %all-to-all-start.1) | async-done | bytes 524320 | tf_op jit(solution)/shard_map/all_to_all | solution.py:96
  109.4 62.8 %while.16 = (s32[]{:T(128)}, f32[32,64,128]{2,1,0:T(8,128)S(1)}, f32[32,64,128]{2,1,0:T(8,128)}, f32[8,32]{1,0:T(8,128)S(1)}, f32[8,32]{1,0:T(8,128)S(1)}, /*ind...) while((s32[]{:T(128)}, f32[32,64,128]{2,1,0:T(8,128)S(1)}, ...), condition=%wide.region_2.3_spmd.clone.clone, body=%wide.region_0.2_spmd.clone.clone.sunk | while | flops 140759840 | bytes 18960384 | solution.py:58
  174.6 9.2 %all-to-all-start.3 = ((bf16[64,128,32]{1,2,0:T(8,128)(2,1)}), bf16[64,128,32]{1,2,0:T(8,128)(2,1)}, u32[]{:S(2)}, u32[]{:S(2)}) async-start(bf16[64,128,32]{1,2,0:T(8,128)(2,1)} %copy_bitcast_fusion), calls=%async_computation.3 | async-start | bytes 1048576 | tf_op jit(solution)/shard_map/all_to_all | solution.py:113
  185.0 27.9 %all-to-all-done.3 = bf16[64,128,32]{1,2,0:T(8,128)(2,1)} async-done(((bf16[64,128,32]{1,2,0:T(8,128)(2,1)}), bf16[64,128,32]{1,2,0:T(8,128)(2,1)}, u32[]{:S(2)}, u32[]{:S(2)}) %all-to-all-start.3) | async-done | bytes 524320 | tf_op jit(solution)/shard_map/all_to_all | solution.py:113
  212.9 8.6 %all-to-all-start.2 = ((bf16[64,128,32]{1,2,0:T(8,128)(2,1)}), bf16[64,128,32]{1,2,0:T(8,128)(2,1)S(1)}, u32[]{:S(2)}, u32[]{:S(2)}) async-start(bf16[64,128,32]{1,2,0:T(8,128)(2,1)} %copy_bitcast_fusion.1), calls=%async_computation.2 | async-start | bytes 1048576 | tf_op jit(solution)/shard_map/all_to_all | solution.py:112
  221.6 6.3 %multiply_reduce_fusion.6 = (f32[2048]{0:T(1024)S(1)}, f32[2048]{0:T(1024)S(1)}, f32[2048]{0:T(1024)S(1)}, f32[128,2048]{0,1:T(8,128)}, f32[2048]{0:T(1024)S(1)}...) fusion(f32[130,2048]{0,1:T(8,128)S(1)} %copy-done.3, f32[128,2048]{0,1:T(8,128)} %get-tuple-element.211, ...), kind=kLoop, calls=%fused_computation.106 | loop fusion | flops 3919872 | bytes 11059200 | tf_op jit(solution)/shard_map/reduce_sum | solution.py:136
  228.0 22.9 %all-to-all-done.2 = bf16[64,128,32]{1,2,0:T(8,128)(2,1)S(1)} async-done(((bf16[64,128,32]{1,2,0:T(8,128)(2,1)}), bf16[64,128,32]{1,2,0:T(8,128)(2,1)S(1)}, u32[]{:S(2)}, u32[]{:S(2)}) %all-to-all-start.2) | async-done | bytes 524320 | tf_op jit(solution)/shard_map/all_to_all | solution.py:112
  251.6 4.7 multiply_reduce_fusion.9
  264.8 16.8 %psum.7 = f32[32,8]{0,1:T(8,128)} all-reduce(f32[32,8]{0,1:T(8,128)S(1)} %multiply_bitcast_fusion), channel_id=1, replica_groups=mesh['ctx'=64,'dp'=8] {'dp'}, use_global_device_ids=true, to_apply=%region_3.4 | all-reduce | flops 256 | bytes 2048 | tf_op jit(solution)/shard_map/psum | solution.py:115
  281.6 2.0 copy.43
  285.2 1.6 convert_element_type.100
  288.4 2.7 fusion.74
  291.1 2.0 copy.44
  293.2 4.1 fusion.75
  297.2 2.0 copy.45
  299.3 2.2 fusion.76
  302.5 218.7 %all-gather.3.cloned.1.call-done = f32[1536,3,2048]{2,1,0:T(4,128)} async-done(((f32[3,3,2048]{2,1,0:T(4,128)}), f32[1536,3,2048]{2,1,0:T(4,128)}) %all-gather.3.cloned.1.call-update) | async-done | bytes 37748752 | tf_op jit(solution)/shard_map/all_gather | solution.py:144
  521.2 17.2 %reduce_sum.108 = f32[3,3,2048]{2,1,0:T(4,128)} reduce(f32[512,3,3,2048]{3,2,1,0:T(4,128)} %bitcast.165, f32[]{:T(128)} %constant.8.clone.1), dimensions={0}, to_apply=%region_13.14 | reduce | flops 9418752 | bytes 37822468 | tf_op jit(solution)/shard_map/reduce_sum | solution.py:144
  (203 shorter events, 86.8 us)
Async XLA Ops:
  9.5 7.7 %collective-permute-start = (bf16[3,2,2048]{2,1,0:T(2,128)(2,1)S(1)}, bf16[3,2,2048]{2,1,0:T(2,128)(2,1)S(1)}, u32[]{:S(2)}, u32[]{:S(2)}) collective-permute-start(bf16[3,2,2048]{2,1,0:T(2,128)(2,1)S(1)} %pad_maximum_fusion.4), channel_id=1, source_target_pairs={{0,8},{8,16},{16,24},{24,32},{32,40},{40,48},{48,56},{56,64},{64,7... | collective-permute-start | bytes 73736 | tf_op jit(solution)/shard_map/ppermute | solution.py:13
  18.7 4.5 copy-start.2
  18.7 4.5 copy-start.4
  18.7 22.8 %copy-start.12 = (bf16[1,128,2048]{2,1,0:T(8,128)(2,1)S(1)}, bf16[1,128,2048]{2,1,0:T(8,128)(2,1)}, u32[]{:S(2)}) copy-start(bf16[1,128,2048]{2,1,0:T(8,128)(2,1)} %param.9) | copy-start | bytes 1572868
  23.2 18.6 %copy-start.13 = (bf16[1,128,2048]{2,1,0:T(8,128)(2,1)S(1)}, bf16[1,128,2048]{2,1,0:T(8,128)(2,1)}, u32[]{:S(2)}) copy-start(bf16[1,128,2048]{2,1,0:T(8,128)(2,1)} %param.12) | copy-start | bytes 1572868
  23.2 47.5 %all-to-all-start = ((bf16[128,64,32]{0,2,1:T(8,128)(2,1)}), bf16[128,64,32]{0,2,1:T(8,128)(2,1)S(1)}, u32[]{:S(2)}, u32[]{:S(2)}) async-start(bf16[128,64,32]{0,2,1:T(8,128)(2,1)} %bitcast.16), calls=%async_computation | async-start | bytes 1048576 | tf_op jit(solution)/shard_map/all_to_all | solution.py:95
  42.1 4.5 copy-start.9
  44.2 35.2 %copy-start.14 = (f32[8]{0:T(128)S(1)}, f32[8]{0:T(128)}, u32[]{:S(2)}) copy-start(f32[8]{0:T(128)} %param.15) | copy-start | bytes 100
  70.8 37.6 %all-to-all-start.1 = ((bf16[128,64,32]{0,2,1:T(8,128)(2,1)}), bf16[128,64,32]{0,2,1:T(8,128)(2,1)S(1)}, u32[]{:S(2)}, u32[]{:S(2)}) async-start(bf16[128,64,32]{0,2,1:T(8,128)(2,1)} %bitcast.20), calls=%async_computation.1 | async-start | bytes 1048576 | tf_op jit(solution)/shard_map/all_to_all | solution.py:96
  112.9 2.0 copy-start
  128.6 2.0 copy-start
  136.4 2.0 copy-start
  144.2 2.0 copy-start
  152.1 2.0 copy-start
  159.9 2.0 copy-start
  167.8 2.0 copy-start
  174.6 38.3 %all-to-all-start.3 = ((bf16[64,128,32]{1,2,0:T(8,128)(2,1)}), bf16[64,128,32]{1,2,0:T(8,128)(2,1)}, u32[]{:S(2)}, u32[]{:S(2)}) async-start(bf16[64,128,32]{1,2,0:T(8,128)(2,1)} %copy_bitcast_fusion), calls=%async_computation.3 | async-start | bytes 1048576 | tf_op jit(solution)/shard_map/all_to_all | solution.py:113
  183.8 37.8 %copy-start.3 = (f32[130,2048]{0,1:T(8,128)S(1)}, f32[130,2048]{0,1:T(8,128)}, u32[]{:S(2)}) copy-start(f32[130,2048]{0,1:T(8,128)} %copy-done.2) | copy-start | bytes 3194884
  212.9 37.9 %all-to-all-start.2 = ((bf16[64,128,32]{1,2,0:T(8,128)(2,1)}), bf16[64,128,32]{1,2,0:T(8,128)(2,1)S(1)}, u32[]{:S(2)}, u32[]{:S(2)}) async-start(bf16[64,128,32]{1,2,0:T(8,128)(2,1)} %copy_bitcast_fusion.1), calls=%async_computation.2 | async-start | bytes 1048576 | tf_op jit(solution)/shard_map/all_to_all | solution.py:112
  221.5 299.6 %all-gather.3.cloned.1.call-start = ((), (), s32[]{:S(2)}) async-start(), calls=%async_computation.4 | async-start | bytes 50429952 | tf_op jit(solution)/shard_map/all_gather | solution.py:144
  251.6 5.4 copy-start.7
  256.3 2.8 copy-start.8
  263.4 20.3 %collective-permute-start.1 = (bf16[3,2,2048]{2,1,0:T(2,128)(2,1)S(1)}, bf16[3,2,2048]{2,1,0:T(2,128)(2,1)S(1)}, u32[]{:S(2)}, u32[]{:S(2)}) collective-permute-start(bf16[3,2,2048]{2,1,0:T(2,128)(2,1)S(1)} %pad_maximum_fusion.5), channel_id=1, source_target_pairs={{8,0},{16,8},{24,16},{32,24},{40,32},{48,40},{56,48},{64,56},{72,6... | collective-permute-start | bytes 73736 | tf_op jit(solution)/shard_map/ppermute | solution.py:13
  293.2 6.1 %copy-start.10 = (f32[2,2048]{0,1:T(8,128)S(1)}, f32[2,2048]{0,1:T(8,128)}, u32[]{:S(2)}) copy-start(f32[2,2048]{0,1:T(8,128)} %get-tuple-element.220) | copy-start | bytes 49156
  (12 other events, 12.7 us)
Sparse Core Ops, SparseCore 0:
  257.1 263.9 all-gather.2
